TPU v7x, 256 devices: a whole 4x4x8 slice. The times are simulated.
256 devices in a mesh: section: 16 (over x, y), tensor: 16 (over z, core).
Axes of the slice: x: 4, y: 4, z: 8, core: 2. Of those that a mesh axis runs over, the one named last changes fastest.
Arguments:
- queries: bfloat16 [16, 512, 8192], P('section', None, 'tensor'), may hold values from -20 to 20
- key_rows: bfloat16 [16, 512, 1024], P('section'), may hold values from -6 to 6
- value_rows: bfloat16 [16, 512, 1024], P('section'), may hold values from -6 to 6
- out_grad: bfloat16 [16, 512, 8192], P('section', None, 'tensor'), may hold values from -24 to 24
- layer_input: bfloat16 [16, 512, 8192], P('section', 'tensor'), may hold values from -64 to 64
- query_weight: bfloat16 [16, 8192, 8192], P('section', None, 'tensor'), may hold values from -0.0625 to 0.0625
- dion_basis: float32 [16, 8192, 256], P('section', 'tensor'), may hold values from -0.0625 to 0.0625
- lengths: int32 [16, 3], P('section'), may hold values from 1 to 256, 512 in all within a row
Outputs:
- upstream: bfloat16 [16, 512, 8192], P('section', 'tensor')
- left_factor: float32 [16, 8192, 256], P('section', 'tensor')
- right_factor: float32 [16, 8192, 256], P('section', 'tensor')
Inputs may be any that keep to these rules, and one draw needn't show every extreme that they name: For each section the lengths of the prompt, the chosen and the rejected response, in that order, summing to 512.
All inputs are finite; a program needn't handle non-finite values.
Results may differ from a plain program's by a relative error of at most 0.022.
Values may be sent and summed in bfloat16 or wider, within the bound.
No kernel may reach another device: no remote copies, remote signals or barrier semaphores. Data moves between devices by JAX's collectives and lax.ppermute only.
A program may use at most 64 MiB of HBM per device.

v0:
```python
import math
import jax
import jax.numpy as jnp
from jax import lax
from jax.sharding import PartitionSpec as P

D = 8192
HD = 128
GROUP = 8
rope_base = 500000.0
highest = lax.Precision.HIGHEST


def shifted(value, axis, steps):
    count = lax.axis_size(axis)
    first, last = (max(0, -steps), min(count, count - steps))
    return lax.ppermute(value, axis, [(source, source + steps) for source in range(first, last)])


def tree_layout(lengths_row, token_count):
    token_ids = jnp.arange(token_count, dtype=jnp.int32)
    bound_one = lengths_row[0]
    bound_two = lengths_row[0] + lengths_row[1]
    positions = jnp.where(token_ids < bound_two, token_ids, token_ids - lengths_row[1]).astype(
        jnp.float32
    )
    row_ids = token_ids[:, None]
    col_ids = token_ids[None, :]
    crossed = (row_ids >= bound_two) & (col_ids >= bound_one) & (col_ids < bound_two)
    visible = (col_ids <= row_ids) & jnp.logical_not(crossed)
    return (positions, visible)


def unrotate(rotated, positions):
    head_dim = rotated.shape[-1]
    half_dim = head_dim // 2
    freq_ids = jnp.arange(half_dim, dtype=jnp.float32)
    inverse = jnp.exp(-math.log(rope_base) * 2.0 * freq_ids / head_dim)
    angles = positions[:, None] * inverse[None, :]
    cosine = jnp.cos(angles)[:, None, :]
    sine_part = jnp.sin(angles)[:, None, :]
    first_half = rotated[..., :half_dim]
    second_half = rotated[..., half_dim:]
    return jnp.concatenate(
        [
            first_half * cosine + second_half * sine_part,
            second_half * cosine - first_half * sine_part,
        ],
        axis=-1,
    )


def local_backward(query_heads, grad_heads, key_block, value_block, visible):
    score_scale = 1.0 / math.sqrt(query_heads.shape[-1])
    scores = (
        jnp.einsum("qhd,kd->hqk", query_heads, key_block, preferred_element_type=jnp.float32)
        * score_scale
    )
    scores = jnp.where(visible[None], scores, -jnp.inf)
    row_max = jnp.max(scores, axis=-1, keepdims=True)
    exp_scores = jnp.exp(scores - row_max)
    weights = exp_scores / jnp.sum(exp_scores, axis=-1, keepdims=True)
    weights_low = weights.astype(jnp.bfloat16)
    outputs = jnp.einsum(
        "hqk,kd->qhd", weights_low, value_block, preferred_element_type=jnp.float32
    )
    out_dot = jnp.sum(grad_heads.astype(jnp.float32) * outputs, axis=-1)
    prob_grad = jnp.einsum(
        "qhd,kd->hqk", grad_heads, value_block, preferred_element_type=jnp.float32
    )
    score_grad = (weights * (prob_grad - out_dot.T[:, :, None])).astype(jnp.bfloat16)
    return (
        jnp.einsum("hqk,kd->qhd", score_grad, key_block, preferred_element_type=jnp.float32)
        * score_scale
    )


def local(queries, key_rows, value_rows, out_grad, layer_input, query_weight, dion_basis, lengths):
    token_count = queries.shape[1]
    local_width = queries.shape[2]
    local_heads = local_width // HD
    tensor_count = lax.axis_size("tensor")
    tensor_index = lax.axis_index("tensor")
    col_width = D // tensor_count
    gathered = lax.all_gather(layer_input[0], "tensor", axis=0, tiled=True)
    columns = lax.dynamic_slice_in_dim(gathered, tensor_index * col_width, col_width, 1)
    positions, visible = tree_layout(lengths[0], token_count)
    group_head = tensor_index * local_heads // GROUP
    key_block = lax.dynamic_slice_in_dim(key_rows[0], group_head * HD, HD, 1)
    value_block = lax.dynamic_slice_in_dim(value_rows[0], group_head * HD, HD, 1)
    rotated = local_backward(
        queries[0].reshape(token_count, local_heads, HD),
        out_grad[0].reshape(token_count, local_heads, HD),
        key_block,
        value_block,
        visible,
    )
    query_grad = unrotate(rotated, positions).reshape(token_count, local_width).astype(jnp.bfloat16)
    weight_local = query_weight[0]
    layer_grad = lax.psum_scatter(
        lax.dot_general(
            query_grad, weight_local, (((1,), (1,)), ((), ())), preferred_element_type=jnp.float32
        ).astype(jnp.bfloat16),
        "tensor",
        scatter_dimension=0,
        tiled=True,
    )
    upstream = shifted(layer_grad, "section", -1)
    grad_wide = query_grad.astype(jnp.float32)
    projected = lax.psum(jnp.dot(grad_wide, dion_basis[0], precision=highest), "tensor")
    column_wide = columns.astype(jnp.float32)
    left_raw = lax.dot_general(column_wide, projected, (((0,), (0,)), ((), ())), precision=highest)
    gram_part = lax.dot_general(left_raw, left_raw, (((0,), (0,)), ((), ())), precision=highest)
    mixed_part = jnp.dot(column_wide, left_raw, precision=highest)
    gram_total, mixed_total = lax.psum((gram_part, mixed_part), "tensor")
    lower_factor = jnp.linalg.cholesky(gram_total)
    left_orth = lax.linalg.triangular_solve(
        lower_factor, left_raw, left_side=False, lower=True, transpose_a=True
    )
    mixed_orth = lax.linalg.triangular_solve(
        lower_factor, mixed_total, left_side=False, lower=True, transpose_a=True
    )
    right_factor = lax.dot_general(
        grad_wide, mixed_orth, (((0,), (0,)), ((), ())), precision=highest
    )
    return (upstream[None], (left_orth * math.sqrt(D))[None], right_factor[None])


def solution(mesh):
    placed = (
        P("section", None, "tensor"),
        P("section", None, None),
        P("section", None, None),
        P("section", None, "tensor"),
        P("section", "tensor", None),
        P("section", None, "tensor"),
        P("section", "tensor", None),
        P("section", None),
    )
    return jax.shard_map(
        local,
        mesh=mesh,
        in_specs=placed,
        out_specs=(
            P("section", "tensor", None),
            P("section", "tensor", None),
            P("section", "tensor", None),
        ),
        check_vma=False,
    )
```

profile of v0, /device:TPU:26, one launch (start us, length us, event | category | flops | bytes accessed | tf_op | source)
XLA Modules:
  0.0 409.4 jit_solution(8106175779800506039)
XLA Ops:
  7.2 1.3 fusion.63
  11.2 1.2 reshape_squeeze.6
  12.4 0.7 fusion.27
  13.4 2.1 fusion.64
  15.5 1.9 copy-done.3
  17.4 1.4 fusion.5
  19.2 1.2 reshape_squeeze.7
  21.1 3.5 fusion.12
  25.4 1.5 fusion.19
  27.0 0.7 all-gather.3.cloned.1.call-update
  27.7 111.7 %all-reduce.5.cloned.1.call-done = f32[512,256]{1,0:T(8,128)} async-done(((f32[512,256]{1,0:T(8,128)}), f32[512,256]{1,0:T(8,128)}) %all-reduce.5.cloned.1.call-update) | async-done | bytes 524304 | tf_op jit(solution)/shard_map/psum | solution.py:110
  139.4 58.2 %all-gather.3.cloned.1.call-done = bf16[1,512,8192]{2,1,0:T(8,128)(2,1)} async-done(((bf16[1,32,8192]{2,1,0:T(8,128)(2,1)}), bf16[1,512,8192]{2,1,0:T(8,128)(2,1)}) %all-gather.3.cloned.1.call-update) | async-done | bytes 8388624 | tf_op jit(solution)/shard_map/all_gather | solution.py:85
  197.7 1.9 fusion.23
  199.6 1.7 fusion.65
  201.3 2.5 fusion.21
  203.9 10.2 %convolution_convert_fusion = bf16[512,8192]{1,0:T(8,128)(2,1)} fusion(bf16[512,512]{0,1:T(8,128)(2,1)S(1)} %bitcast.114, bf16[1,8192,512]{2,1,0:T(8,128)(2,1)} %param.15), kind=kOutput, calls=%fused_computation.3 | convolution fusion | flops 4299161600 | bytes 17301504 | tf_op jit(solution)/shard_map/dot_general | solution.py:101
  214.1 99.1 %all-reduce.7.cloned.1.call-done = (f32[256,256]{0,1:T(8,128)}, f32[512,256]{1,0:T(8,128)}) async-done(((f32[256,256]{0,1:T(8,128)}, f32[512,256]{1,0:T(8,128)}), (f32[256,256]{0,1:T(8,128)}, f32[512,256]{1,0:T(8,128)})) %all-reduce.7.cloned.1.call-update) | async-done | bytes 786448 | tf_op jit(solution)/shard_map/psum | solution.py:115
  313.3 1.1 copy.22
  314.4 1.0 fusion.35
  315.4 11.7 %cholesky.50 = f32[128,128]{1,0:T(8,128)S(1)} custom-call(f32[128,128]{1,0:T(8,128)S(1)} %cholesky.118), custom_call_target="Cholesky" | custom-call | tf_op jit(solution)/shard_map/jit(cholesky)/cholesky | solution.py:116
  327.2 9.8 %custom-call.14 = f32[1,128,128]{1,2,0:T(8,128)S(1)} custom-call(f32[1,128,128]{2,1,0:T(8,128)S(1)} %get-tuple-element.43), custom_call_target="InvertDiagBlocksLowerTriangular" | custom-call | tf_op jit(solution)/shard_map/jit(cholesky)/cholesky | solution.py:116
  337.5 11.7 %cholesky.105 = f32[128,128]{1,0:T(8,128)S(1)} custom-call(f32[128,128]{1,0:T(8,128)S(1)} %convolution_subtract_fusion.2), custom_call_target="Cholesky" | custom-call | tf_op jit(solution)/shard_map/jit(cholesky)/cholesky | solution.py:116
  351.9 4.0 while.4
  352.5 1.4 bitcast_dynamic-update-slice_fusion.2
  354.5 1.4 bitcast_dynamic-update-slice_fusion.2
  355.9 19.9 %custom-call.16 = f32[2,128,128]{1,2,0:T(8,128)S(1)} custom-call(f32[2,128,128]{2,1,0:T(8,128)S(1)} %get-tuple-element.18), custom_call_target="InvertDiagBlocksLowerTriangular" | custom-call | tf_op jit(solution)/shard_map/triangular_solve/custom-call.0 | solution.py:117
  377.3 1.0 copy.23
  378.8 8.2 %reduce-scatter.2.cloned.1.call-done = bf16[32,8192]{1,0:T(8,128)(2,1)} async-done(((bf16[512,8192]{1,0:T(8,128)(2,1)}), bf16[32,8192]{1,0:T(8,128)(2,1)}) %reduce-scatter.2.cloned.1.call-update) | async-done | bytes 524304 | tf_op jit(solution)/shard_map/reduce_scatter | solution.py:100
  387.0 2.8 collective-permute-start
  390.8 1.4 convolution_bitcast_fusion
  392.2 9.8 %collective-permute-done = bf16[32,8192]{1,0:T(8,128)(2,1)S(1)} collective-permute-done((bf16[32,8192]{1,0:T(8,128)(2,1)}, bf16[32,8192]{1,0:T(8,128)(2,1)S(1)}, u32[]{:S(2)}, u32[]{:S(2)}) %collective-permute-start) | collective-permute-done | bytes 524320 | tf_op jit(solution)/shard_map/ppermute | solution.py:17
  402.1 0.8 copy.50
  (48 shorter events, 9.6 us)
Async XLA Ops:
  7.2 5.2 %copy-start = (bf16[1,512,1024]{2,1,0:T(8,128)(2,1)S(1)}, bf16[1,512,1024]{2,1,0:T(8,128)(2,1)}, u32[]{:S(2)}) copy-start(bf16[1,512,1024]{2,1,0:T(8,128)(2,1)} %param.11) | copy-start | bytes 3145732
  7.2 132.2 %all-reduce.5.cloned.1.call-start = ((), (), s32[]{:S(2)}) async-start(), calls=%async_computation.2 | async-start | bytes 1048576 | tf_op jit(solution)/shard_map/psum | solution.py:110
  15.5 1.9 copy-start.3
  21.1 4.2 %copy-start.1 = (f32[1,512,256]{2,1,0:T(8,128)S(1)}, f32[1,512,256]{2,1,0:T(8,128)}, u32[]{:S(2)}) copy-start(f32[1,512,256]{2,1,0:T(8,128)} %param.16) | copy-start | bytes 1572868
  26.9 170.7 %all-gather.3.cloned.1.call-start = ((), (), s32[]{:S(2)}) async-start(), calls=%async_computation.3 | async-start | bytes 8912896 | tf_op jit(solution)/shard_map/all_gather | solution.py:85
  27.7 285.6 %all-reduce.7.cloned.1.call-start = ((), (), s32[]{:S(2)}) async-start(), calls=%async_computation.4 | async-start | bytes 1572864 | tf_op jit(solution)/shard_map/psum | solution.py:115
  203.8 183.2 %reduce-scatter.2.cloned.1.call-start = ((), (), s32[]{:S(2)}) async-start(), calls=%async_computation.1 | async-start | bytes 8912896 | tf_op jit(solution)/shard_map/reduce_scatter | solution.py:100
  313.3 65.1 %copy-start.2 = (f32[512,256]{1,0:T(8,128)S(1)}, f32[512,256]{1,0:T(8,128)}, u32[]{:S(2)}) copy-start(f32[512,256]{1,0:T(8,128)} %get-tuple-element.35) | copy-start | bytes 1572868
  387.0 15.1 %collective-permute-start = (bf16[32,8192]{1,0:T(8,128)(2,1)}, bf16[32,8192]{1,0:T(8,128)(2,1)S(1)}, u32[]{:S(2)}, u32[]{:S(2)}) collective-permute-start(bf16[32,8192]{1,0:T(8,128)(2,1)} %reduce-scatter.2.cloned.1.call-done), channel_id=1, source_target_pairs={{16,0},{32,16},{48,32},{64,48},{80,64},{96,80},{112,96},{128,112},... | collective-permute-start | bytes 1572872 | tf_op jit(solution)/shard_map/ppermute | solution.py:17
Sparse Core Ops, SparseCore 0:
  27.1 112.3 all-reduce.4
  141.4 56.2 all-gather.2
  203.9 109.2 all-reduce.6
  315.7 71.2 reduce-scatter.1
where the time goes:
time: 410 us; the launch traced here: 409 us
  waiting for transfers between devices  288 us (70%)
  other arithmetic  60.6 us (15%)
  matrix products  28.2 us (7%)
  between operations  16.7 us (4%)
  local copies, waits for them, and re-layouts  13.1 us (3%)
    psum x1, waiting for transfers between devices, local(): lax.psum(jnp.dot(grad_wide, dion_basis[0], precision=highest), 'tensor')  112 us
    psum x1, waiting for transfers between devices, local(): gram_total, mixed_total = lax.psum((gram_part, mixed_part), 'tensor')  99.1 us
    all_gather x1, waiting for transfers between devices, local(): gathered = lax.all_gather(layer_input[0], 'tensor', axis=0, tiled=True)  58.2 us
    another operation x7, other arithmetic, local(): lower_factor = jnp.linalg.cholesky(gram_total)  34.6 us
    another operation x4, other arithmetic, local(): lax.linalg.triangular_solve(lower_factor, left_raw, left_side=False, lowe...  19.9 us
    dot_general x1, matrix products, local(): lax.dot_general(query_grad, weight_local, (((1,), (1,)), ((), ())), prefe...  10.2 us
    ppermute x1, waiting for transfers between devices, shifted(): lax.ppermute(value, axis, [(source, source + steps) for source in range(f...  9.81 us
    reduce_scatter x1, waiting for transfers between devices, local(): lax.psum_scatter(lax.dot_general(query_grad, weight_local, (((1,), (1,)),...  8.25 us
  transfers between devices with their start and end apart: 5, of which 5 were waited for; matrix products, arithmetic and copies ran while one was open for 19% of the time, Pallas kernels for 0%

commit v1 on v0

--- a/solution.py
+++ b/solution.py
@@ -3,6 +3,7 @@
 import jax.numpy as jnp
 from jax import lax
 from jax.sharding import PartitionSpec as P
+from jax.lax import all_to_all, axis_size
 
 D = 8192
 HD = 128
@@ -82,7 +83,10 @@
     tensor_count = lax.axis_size("tensor")
     tensor_index = lax.axis_index("tensor")
     col_width = D // tensor_count
-    gathered = lax.all_gather(layer_input[0], "tensor", axis=0, tiled=True)
+    slab_in = layer_input[0]
+    gathered = jnp.concatenate(
+        all_to_all(jnp.stack([slab_in for _ in range(axis_size("tensor"))]), "tensor", 0, 0), 0
+    )
     columns = lax.dynamic_slice_in_dim(gathered, tensor_index * col_width, col_width, 1)
     positions, visible = tree_layout(lengths[0], token_count)
     group_head = tensor_index * local_heads // GROUP

time: 410 us -> 445 us (1.085)
  waiting for transfers between devices: 288 us -> 311 us
  starting transfers between devices: 2.95 us -> 11.3 us
    psum x1, waiting for transfers between devices: 112 us -> 192 us  [local(): lax.psum(jnp.dot(grad_wide, dion_basis[0], precision=highest), 'tensor')]
    all_gather x1 -> x0, waiting for transfers between devices: 58.2 us -> none  [local(): gathered = lax.all_gather(layer_input[0], 'tensor', axis=0, tiled=True)]
    all_to_all x0 -> x1, starting transfers between devices: none -> 8.75 us  [local(): all_to_all(jnp.stack([slab_in for _ in range(axis_size('tensor'))]), 'ten...]
    another operation x0 -> x1, local copies, waits for them, and re-layouts: none -> 5.38 us  [local(): jnp.stack([slab_in for _ in range(axis_size('tensor'))])]
  transfers between devices with their start and end apart: 5 -> 5, of which waited for: 5 -> 4; matrix products, arithmetic and copies ran while one was open for 19% -> 21% of each run, Pallas kernels for 0% -> 0%
where the time goes in v1:
time: 445 us; the launch traced here: 444 us
  waiting for transfers between devices  311 us (70%)
  other arithmetic  60.6 us (14%)
  matrix products  28.2 us (6%)
  local copies, waits for them, and re-layouts  16.7 us (4%)
  between operations  16.7 us (4%)
  starting transfers between devices  11.3 us (3%)
    psum x1, waiting for transfers between devices, local(): lax.psum(jnp.dot(grad_wide, dion_basis[0], precision=highest), 'tensor')  192 us
    psum x1, waiting for transfers between devices, local(): gram_total, mixed_total = lax.psum((gram_part, mixed_part), 'tensor')  101 us
    another operation x7, other arithmetic, local(): lower_factor = jnp.linalg.cholesky(gram_total)  34.6 us
    another operation x4, other arithmetic, local(): lax.linalg.triangular_solve(lower_factor, left_raw, left_side=False, lowe...  19.9 us
    dot_general x1, matrix products, local(): lax.dot_general(query_grad, weight_local, (((1,), (1,)), ((), ())), prefe...  10.2 us
    ppermute x1, waiting for transfers between devices, shifted(): lax.ppermute(value, axis, [(source, source + steps) for source in range(f...  10 us
  transfers between devices with their start and end apart: 5, of which 4 were waited for; matrix products, arithmetic and copies ran while one was open for 21% of the time, Pallas kernels for 0%

profile of v1, /device:TPU:26, one launch (start us, length us, event | category | flops | bytes accessed | tf_op | source)
XLA Modules:
  0.0 444.4 jit_solution(4569880823112886271)
XLA Ops:
  7.2 5.4 %stack.3 = bf16[16,32,8192]{2,1,0:T(8,128)(2,1)} broadcast(bf16[32,8192]{1,0:T(8,128)(2,1)} %bitcast.116), dimensions={1,2} | broadcast | bytes 8912896 | tf_op jit(solution)/shard_map/stack | solution.py:88
  12.6 8.8 %all-to-all-start = ((bf16[16,32,8192]{2,1,0:T(8,128)(2,1)}), bf16[16,32,8192]{2,1,0:T(8,128)(2,1)}, u32[]{:S(2)}, u32[]{:S(2)}) async-start(bf16[16,32,8192]{2,1,0:T(8,128)(2,1)} %stack.3), calls=%async_computation.1 | async-start | bytes 16777216 | tf_op jit(solution)/shard_map/all_to_all | solution.py:88
  23.4 0.7 iota_compare_fusion.5
  24.4 0.7 fusion.23
  25.1 2.1 fusion.62
  27.2 1.9 copy-done.5
  29.2 1.4 fusion.5
  30.9 1.2 reshape_squeeze.7
  32.9 0.7 select_convert_fusion
  34.1 3.5 fusion.12
  37.8 1.5 fusion.19
  39.4 191.8 %all-reduce.5.cloned.1.call-done = f32[512,256]{1,0:T(8,128)} async-done(((f32[512,256]{1,0:T(8,128)}), f32[512,256]{1,0:T(8,128)}) %all-reduce.5.cloned.1.call-update) | async-done | bytes 524304 | tf_op jit(solution)/shard_map/psum | solution.py:114
  231.2 1.9 fusion.27
  233.1 2.5 fusion.25
  235.6 1.7 fusion.63
  237.4 10.2 %convolution_convert_fusion = bf16[512,8192]{1,0:T(8,128)(2,1)} fusion(bf16[512,512]{0,1:T(8,128)(2,1)S(1)} %bitcast.111, bf16[1,8192,512]{2,1,0:T(8,128)(2,1)} %param.15), kind=kOutput, calls=%fused_computation.3 | convolution fusion | flops 4299161600 | bytes 17301504 | tf_op jit(solution)/shard_map/dot_general | solution.py:105
  247.7 100.5 %all-reduce.7.cloned.1.call-done = (f32[256,256]{0,1:T(8,128)}, f32[512,256]{1,0:T(8,128)}) async-done(((f32[256,256]{0,1:T(8,128)}, f32[512,256]{1,0:T(8,128)}), (f32[256,256]{0,1:T(8,128)}, f32[512,256]{1,0:T(8,128)})) %all-reduce.7.cloned.1.call-update) | async-done | bytes 786448 | tf_op jit(solution)/shard_map/psum | solution.py:119
  348.2 1.1 copy.22
  349.3 1.0 fusion.33
  350.3 11.7 %cholesky.50 = f32[128,128]{1,0:T(8,128)S(1)} custom-call(f32[128,128]{1,0:T(8,128)S(1)} %cholesky.118), custom_call_target="Cholesky" | custom-call | tf_op jit(solution)/shard_map/jit(cholesky)/cholesky | solution.py:120
  362.1 9.8 %custom-call.14 = f32[1,128,128]{1,2,0:T(8,128)S(1)} custom-call(f32[1,128,128]{2,1,0:T(8,128)S(1)} %get-tuple-element.43), custom_call_target="InvertDiagBlocksLowerTriangular" | custom-call | tf_op jit(solution)/shard_map/jit(cholesky)/cholesky | solution.py:120
  372.4 11.7 %cholesky.105 = f32[128,128]{1,0:T(8,128)S(1)} custom-call(f32[128,128]{1,0:T(8,128)S(1)} %convolution_subtract_fusion.2), custom_call_target="Cholesky" | custom-call | tf_op jit(solution)/shard_map/jit(cholesky)/cholesky | solution.py:120
  386.9 4.0 while.4
  387.4 1.4 bitcast_dynamic-update-slice_fusion.2
  389.4 1.4 bitcast_dynamic-update-slice_fusion.2
  390.8 19.9 %custom-call.16 = f32[2,128,128]{1,2,0:T(8,128)S(1)} custom-call(f32[2,128,128]{2,1,0:T(8,128)S(1)} %get-tuple-element.18), custom_call_target="InvertDiagBlocksLowerTriangular" | custom-call | tf_op jit(solution)/shard_map/triangular_solve/custom-call.0 | solution.py:121
  412.3 1.0 copy.23
  413.7 8.5 %reduce-scatter.2.cloned.1.call-done = bf16[32,8192]{1,0:T(8,128)(2,1)} async-done(((bf16[512,8192]{1,0:T(8,128)(2,1)}), bf16[32,8192]{1,0:T(8,128)(2,1)}) %reduce-scatter.2.cloned.1.call-update) | async-done | bytes 524304 | tf_op jit(solution)/shard_map/reduce_scatter | solution.py:104
  422.2 2.5 collective-permute-start
  425.6 1.4 convolution_bitcast_fusion
  427.1 10.0 %collective-permute-done = bf16[32,8192]{1,0:T(8,128)(2,1)S(1)} collective-permute-done((bf16[32,8192]{1,0:T(8,128)(2,1)}, bf16[32,8192]{1,0:T(8,128)(2,1)S(1)}, u32[]{:S(2)}, u32[]{:S(2)}) %collective-permute-start) | collective-permute-done | bytes 524320 | tf_op jit(solution)/shard_map/ppermute | solution.py:18
  437.1 0.8 copy.50
  (52 shorter events, 9.0 us)
Async XLA Ops:
  7.2 17.2 %copy-start = (bf16[1,512,1024]{2,1,0:T(8,128)(2,1)S(1)}, bf16[1,512,1024]{2,1,0:T(8,128)(2,1)}, u32[]{:S(2)}) copy-start(bf16[1,512,1024]{2,1,0:T(8,128)(2,1)} %param.11) | copy-start | bytes 3145732
  12.6 8.8 %copy-start.2 = (bf16[1,512,512]{2,1,0:T(8,128)(2,1)S(1)}, bf16[1,512,512]{2,1,0:T(8,128)(2,1)}, u32[]{:S(2)}) copy-start(bf16[1,512,512]{2,1,0:T(8,128)(2,1)} %param.10) | copy-start | bytes 1572868
  12.6 9.0 %copy-start.4 = (s32[1,3]{1,0:T(1,128)S(1)}, s32[1,3]{1,0:T(1,128)}, u32[]{:S(2)}) copy-start(s32[1,3]{1,0:T(1,128)} %param.17) | copy-start | bytes 40
  12.6 218.6 %all-to-all-start = ((bf16[16,32,8192]{2,1,0:T(8,128)(2,1)}), bf16[16,32,8192]{2,1,0:T(8,128)(2,1)}, u32[]{:S(2)}, u32[]{:S(2)}) async-start(bf16[16,32,8192]{2,1,0:T(8,128)(2,1)} %stack.3), calls=%async_computation.1 | async-start | bytes 16777216 | tf_op jit(solution)/shard_map/all_to_all | solution.py:88
  21.3 209.9 %all-reduce.5.cloned.1.call-start = ((), (), s32[]{:S(2)}) async-start(), calls=%async_computation.3 | async-start | bytes 1048576 | tf_op jit(solution)/shard_map/psum | solution.py:114
  27.2 1.9 copy-start.5
  34.1 3.7 copy-start.1
  39.3 308.9 %all-reduce.7.cloned.1.call-start = ((), (), s32[]{:S(2)}) async-start(), calls=%async_computation.4 | async-start | bytes 1572864 | tf_op jit(solution)/shard_map/psum | solution.py:119
  237.3 184.8 %reduce-scatter.2.cloned.1.call-start = ((), (), s32[]{:S(2)}) async-start(), calls=%async_computation.2 | async-start | bytes 8912896 | tf_op jit(solution)/shard_map/reduce_scatter | solution.py:104
  348.2 65.1 %copy-start.3 = (f32[512,256]{1,0:T(8,128)S(1)}, f32[512,256]{1,0:T(8,128)}, u32[]{:S(2)}) copy-start(f32[512,256]{1,0:T(8,128)} %get-tuple-element.35) | copy-start | bytes 1572868
  422.2 14.9 %collective-permute-start = (bf16[32,8192]{1,0:T(8,128)(2,1)}, bf16[32,8192]{1,0:T(8,128)(2,1)S(1)}, u32[]{:S(2)}, u32[]{:S(2)}) collective-permute-start(bf16[32,8192]{1,0:T(8,128)(2,1)} %reduce-scatter.2.cloned.1.call-done), channel_id=1, source_target_pairs={{16,0},{32,16},{48,32},{64,48},{80,64},{96,80},{112,96},{128,112},... | collective-permute-start | bytes 1572872 | tf_op jit(solution)/shard_map/ppermute | solution.py:18
Sparse Core Ops, SparseCore 0:
  39.5 191.6 all-reduce.4
  237.5 110.6 all-reduce.6
  350.8 71.3 reduce-scatter.1
